TPU v7x, 256 devices: a whole 4x4x8 slice. The times are simulated.
256 devices in a mesh: ctx: 64 (over z, x_hi, y), tp: 4 (over x_lo, core).
Axes of the slice: x: 4 (x_hi: 2, x_lo: 2; x = x_hi * 2 + x_lo), y: 4, z: 8, core: 2. Of those that a mesh axis runs over, the one named last changes fastest.
Arguments:
- hit_features: bfloat16 [24576, 1024], P('ctx', 'tp'), may hold values from -6 to 6
- segment: int32 [24576], P('ctx'), may hold values from 0 to 31, never falling along the last dimension, each value on 1 to 1537 neighbouring positions
- norm1_gain: float32 [1024], replicated, may hold values from 0.1 to 1.9
- w_qkv: bfloat16 [3, 1024, 1024], P(None, None, 'tp'), may hold values from -2 to 2
- w_out: bfloat16 [1024, 1024], P('tp'), may hold values from -0.1875 to 0.1875
- norm2_gain: float32 [1024], replicated, may hold values from 0.1 to 1.9
- w_up: bfloat16 [1024, 4096], P(None, 'tp'), may hold values from -0.1875 to 0.1875
- w_down: bfloat16 [4096, 1024], P('tp'), may hold values from -0.09375 to 0.09375
Outputs:
- layer_out: bfloat16 [24576, 1024], P('ctx', 'tp')
Inputs may be any that keep to these rules, and one draw needn't show every extreme that they name: `segment`: never falls from one hit to the next; every event number below 32 appears; each event holds 1 to 1537 consecutive hits and some event holds exactly 1537.
All inputs are finite; a program needn't handle non-finite values.
Results may differ from a plain program's by a relative error of at most 0.014.
Values may be sent and summed in bfloat16 or wider, within the bound.
No kernel may reach another device: no remote copies, remote signals or barrier semaphores. Data moves between devices by JAX's collectives and lax.ppermute only.
A program may use at most 128 MiB of HBM per device.

v0:
```python
import jax
import jax.numpy as jnp
from jax import lax
from jax.sharding import PartitionSpec as P

HEAD_DIM = 64
REACH = 4
epsilon = 1e-05
neg_fill = -1e30


def shifted(block, axis, distance):
    devices = range(lax.axis_size(axis))
    route = [(i - distance, i) for i in devices if i - distance in devices]
    return lax.ppermute(block, axis, route)


def rms_scale(features, gain):
    mean_square = jnp.mean(features * features, axis=-1, keepdims=True)
    return features * lax.rsqrt(mean_square + epsilon) * gain


def absorb(carry_state, query_heads, event_tag, key_rows, value_rows, key_tag):
    row_top, row_total, weighted = carry_state
    head_count = query_heads.shape[1]
    key_heads = key_rows.reshape(key_rows.shape[0], head_count, HEAD_DIM)
    value_heads = value_rows.reshape(value_rows.shape[0], head_count, HEAD_DIM)
    scores = jnp.einsum("qhd,khd->hqk", query_heads, key_heads, preferred_element_type=jnp.float32)
    matches = (event_tag[:, None] == key_tag[None, :])[None]
    masked = jnp.where(matches, scores, neg_fill)
    new_top = jnp.maximum(row_top, jnp.max(masked, axis=-1, keepdims=True))
    powered = jnp.where(matches, jnp.exp(masked - new_top), 0.0)
    rescale = jnp.exp(row_top - new_top)
    row_total = row_total * rescale + jnp.sum(powered, axis=-1, keepdims=True)
    weighted = weighted * rescale + jnp.einsum(
        "hqk,khd->hqd",
        powered.astype(jnp.bfloat16),
        value_heads,
        preferred_element_type=jnp.float32,
    )
    return (new_top, row_total, weighted)


def shards(hit_features, segment, norm1_gain, w_qkv, w_out, norm2_gain, w_up, w_down):
    features = lax.all_gather(hit_features, "tp", axis=1, tiled=True).astype(jnp.float32)
    normed = rms_scale(features, norm1_gain).astype(jnp.bfloat16)
    projected = jnp.einsum("td,cde->cte", normed, w_qkv, preferred_element_type=jnp.float32)
    queries = (projected[0] * HEAD_DIM ** (-0.5)).astype(jnp.bfloat16)
    key_rows = projected[1].astype(jnp.bfloat16)
    value_rows = projected[2].astype(jnp.bfloat16)
    hit_count = hit_features.shape[0]
    head_count = w_qkv.shape[2] // HEAD_DIM
    query_heads = queries.reshape(hit_count, head_count, HEAD_DIM)
    event_tag = segment + 1
    carry_state = (
        jnp.full((head_count, hit_count, 1), neg_fill, jnp.float32),
        jnp.zeros((head_count, hit_count, 1), jnp.float32),
        jnp.zeros((head_count, hit_count, HEAD_DIM), jnp.float32),
    )
    carry_state = absorb(carry_state, query_heads, event_tag, key_rows, value_rows, event_tag)
    lower = (key_rows, value_rows, event_tag)
    upper = (key_rows, value_rows, event_tag)
    for offset in range(REACH):
        lower = shifted((lower[0], lower[1], lower[2]), "ctx", 1)
        upper = shifted((upper[0], upper[1], upper[2]), "ctx", -1)
        carry_state = absorb(carry_state, query_heads, event_tag, lower[0], lower[1], lower[2])
        carry_state = absorb(carry_state, query_heads, event_tag, upper[0], upper[1], upper[2])
    row_top, row_total, weighted = carry_state
    mixed_heads = (
        jnp.transpose(weighted / row_total, (1, 0, 2))
        .reshape(hit_count, head_count * HEAD_DIM)
        .astype(jnp.bfloat16)
    )
    attn_part = jnp.dot(mixed_heads, w_out, preferred_element_type=jnp.float32)
    residual = features + lax.psum(attn_part.astype(jnp.bfloat16), "tp").astype(jnp.float32)
    normed_second = rms_scale(residual, norm2_gain).astype(jnp.bfloat16)
    hidden = jax.nn.gelu(
        jnp.dot(normed_second, w_up, preferred_element_type=jnp.float32), approximate=False
    ).astype(jnp.bfloat16)
    ffn_part = jnp.dot(hidden, w_down, preferred_element_type=jnp.float32)
    ffn_share = lax.psum_scatter(
        ffn_part.astype(jnp.bfloat16), "tp", scatter_dimension=1, tiled=True
    ).astype(jnp.float32)
    share_width = ffn_share.shape[1]
    residual_share = lax.dynamic_slice_in_dim(
        residual, lax.axis_index("tp") * share_width, share_width, 1
    )
    return (residual_share + ffn_share).astype(jnp.bfloat16)


def solution(mesh):
    return jax.shard_map(
        shards,
        mesh=mesh,
        in_specs=(
            P("ctx", "tp"),
            P("ctx"),
            P(),
            P(None, None, "tp"),
            P("tp", None),
            P(),
            P(None, "tp"),
            P("tp", None),
        ),
        out_specs=P("ctx", "tp"),
        check_vma=False,
    )
```

profile of v0, /device:TPU:1, one launch (start us, length us, event | category | flops | bytes accessed | tf_op | source)
XLA Modules:
  0.0 243.1 jit_solution(5882714588632567019)
XLA Ops:
  6.5 0.8 broadcast_add_fusion
  7.4 4.0 %collective-permute-start = (s32[384]{0:T(512)S(1)}, s32[384]{0:T(512)S(1)}, u32[]{:S(2)}, u32[]{:S(2)}) collective-permute-start(s32[384]{0:T(512)S(1)} %broadcast_add_fusion), channel_id=1, source_target_pairs={{0,4},{4,8},{8,12},{12,16},{16,20},{20,24},{24,28},{28,32},{32,36}... | collective-permute-start | bytes 4616 | tf_op jit(solution)/shard_map/ppermute | solution.py:15
  11.4 1.3 collective-permute-start.3
  12.7 9.6 %all_gather.3 = bf16[384,1024]{1,0:T(8,128)(2,1)S(1)} all-gather(bf16[384,256]{1,0:T(8,128)(2,1)} %param.8), channel_id=1, replica_groups=mesh['ctx'=64,'tp'=4] {'tp'}, dimensions={1}, use_global_device_ids=true | all-gather | bytes 983040 | tf_op jit(solution)/shard_map/all_gather | solution.py:45
  22.5 4.3 %collective-permute-start.6 = (s32[384]{0:T(512)S(1)}, s32[384]{0:T(512)S(1)}, u32[]{:S(2)}, u32[]{:S(2)}) collective-permute-start(s32[384]{0:T(512)S(1)} %collective-permute-done), channel_id=1, source_target_pairs={{0,4},{4,8},{8,12},{12,16},{16,20},{20,24},{24,28},{28,32},{32,36}... | collective-permute-start | bytes 4616 | tf_op jit(solution)/shard_map/ppermute | solution.py:15
  26.8 1.3 collective-permute-start.9
  28.1 2.5 %convolution_bitcast_fusion = f32[3,384,256]{1,2,0:T(8,128)S(1)} fusion(bf16[3,1024,256]{2,1,0:T(8,128)(2,1)} %param.11, bf16[384,1024]{1,0:T(8,128)(2,1)S(1)} %all_gather.3, f32[1024]{0:T(1024)} %param.10, f32[384]{0:T(512)S(1)} %add_rsqrt_fusion.1), kind=kOutput, calls=%fused_computation.64 | convolution fusion | flops 605552640 | bytes 3544576 | tf_op jit(solution)/shard_map/td,cde->cte/dot_general | solution.py:47
  30.7 4.0 %collective-permute-start.12 = (s32[384]{0:T(512)S(1)}, s32[384]{0:T(512)S(1)}, u32[]{:S(2)}, u32[]{:S(2)}) collective-permute-start(s32[384]{0:T(512)S(1)} %collective-permute-done.6), channel_id=1, source_target_pairs={{0,4},{4,8},{8,12},{12,16},{16,20},{20,24},{24,28},{28,32},{32,36}... | collective-permute-start | bytes 4616 | tf_op jit(solution)/shard_map/ppermute | solution.py:15
  34.7 1.3 collective-permute-start.15
  36.0 4.0 %collective-permute-start.1 = (bf16[384,256]{0,1:T(8,128)(2,1)S(1)}, bf16[384,256]{0,1:T(8,128)(2,1)S(1)}, u32[]{:S(2)}, u32[]{:S(2)}) collective-permute-start(bf16[384,256]{0,1:T(8,128)(2,1)S(1)} %bitcast.263), channel_id=1, source_target_pairs={{0,4},{4,8},{8,12},{12,16},{16,20},{20,24},{24,28},{28,32},{32,36}... | collective-permute-start | bytes 589832 | tf_op jit(solution)/shard_map/ppermute | solution.py:15
  40.0 1.3 collective-permute-start.4
  41.3 1.3 collective-permute-start.5
  42.6 8.3 %collective-permute-start.18 = (s32[384]{0:T(512)S(1)}, s32[384]{0:T(512)S(1)}, u32[]{:S(2)}, u32[]{:S(2)}) collective-permute-start(s32[384]{0:T(512)S(1)} %collective-permute-done.12), channel_id=1, source_target_pairs={{0,4},{4,8},{8,12},{12,16},{16,20},{20,24},{24,28},{28,32},{32,36}... | collective-permute-start | bytes 4616 | tf_op jit(solution)/shard_map/ppermute | solution.py:15
  50.9 1.3 collective-permute-start.21
  52.3 7.6 %collective-permute-start.2 = (bf16[384,256]{0,1:T(8,128)(2,1)S(1)}, bf16[384,256]{0,1:T(8,128)(2,1)S(1)}, u32[]{:S(2)}, u32[]{:S(2)}) collective-permute-start(bf16[384,256]{0,1:T(8,128)(2,1)S(1)} %bitcast.275), channel_id=1, source_target_pairs={{0,4},{4,8},{8,12},{12,16},{16,20},{20,24},{24,28},{28,32},{32,36}... | collective-permute-start | bytes 589832 | tf_op jit(solution)/shard_map/ppermute | solution.py:15
  59.9 1.0 broadcast_compare_fusion.8
  61.5 7.0 %collective-permute-start.7 = (bf16[384,256]{0,1:T(8,128)(2,1)S(1)}, bf16[384,256]{0,1:T(8,128)(2,1)S(1)}, u32[]{:S(2)}, u32[]{:S(2)}) collective-permute-start(bf16[384,256]{0,1:T(8,128)(2,1)S(1)} %collective-permute-done.1), channel_id=1, source_target_pairs={{0,4},{4,8},{8,12},{12,16},{16,20},{20,24},{24,28},{28,32},{32,36}... | collective-permute-start | bytes 589832 | tf_op jit(solution)/shard_map/ppermute | solution.py:15
  68.5 1.3 collective-permute-start.10
  69.8 1.3 collective-permute-start.11
  71.7 8.2 %collective-permute-start.8 = (bf16[384,256]{0,1:T(8,128)(2,1)S(1)}, bf16[384,256]{0,1:T(8,128)(2,1)S(1)}, u32[]{:S(2)}, u32[]{:S(2)}) collective-permute-start(bf16[384,256]{0,1:T(8,128)(2,1)S(1)} %collective-permute-done.2), channel_id=1, source_target_pairs={{0,4},{4,8},{8,12},{12,16},{16,20},{20,24},{24,28},{28,32},{32,36}... | collective-permute-start | bytes 589832 | tf_op jit(solution)/shard_map/ppermute | solution.py:15
  79.9 0.6 select_reduce_fusion.6
  80.6 7.0 %collective-permute-start.13 = (bf16[384,256]{0,1:T(8,128)(2,1)S(1)}, bf16[384,256]{0,1:T(8,128)(2,1)S(1)}, u32[]{:S(2)}, u32[]{:S(2)}) collective-permute-start(bf16[384,256]{0,1:T(8,128)(2,1)S(1)} %collective-permute-done.7), channel_id=1, source_target_pairs={{0,4},{4,8},{8,12},{12,16},{16,20},{20,24},{24,28},{28,32},{32,36}... | collective-permute-start | bytes 589832 | tf_op jit(solution)/shard_map/ppermute | solution.py:15
  87.5 1.3 collective-permute-start.16
  89.4 1.3 collective-permute-start.17
  91.3 4.6 %collective-permute-start.14 = (bf16[384,256]{0,1:T(8,128)(2,1)S(1)}, bf16[384,256]{0,1:T(8,128)(2,1)S(1)}, u32[]{:S(2)}, u32[]{:S(2)}) collective-permute-start(bf16[384,256]{0,1:T(8,128)(2,1)S(1)} %collective-permute-done.8), channel_id=1, source_target_pairs={{0,4},{4,8},{8,12},{12,16},{16,20},{20,24},{24,28},{28,32},{32,36}... | collective-permute-start | bytes 589832 | tf_op jit(solution)/shard_map/ppermute | solution.py:15
  96.0 7.0 %collective-permute-start.19 = (bf16[384,256]{0,1:T(8,128)(2,1)S(1)}, bf16[384,256]{0,1:T(8,128)(2,1)S(1)}, u32[]{:S(2)}, u32[]{:S(2)}) collective-permute-start(bf16[384,256]{0,1:T(8,128)(2,1)S(1)} %collective-permute-done.13), channel_id=1, source_target_pairs={{0,4},{4,8},{8,12},{12,16},{16,20},{20,24},{24,28},{28,32},{32,36}... | collective-permute-start | bytes 589832 | tf_op jit(solution)/shard_map/ppermute | solution.py:15
  103.0 1.3 collective-permute-start.22
  104.3 1.3 collective-permute-start.23
  106.2 4.8 %collective-permute-start.20 = (bf16[384,256]{0,1:T(8,128)(2,1)S(1)}, bf16[384,256]{0,1:T(8,128)(2,1)S(1)}, u32[]{:S(2)}, u32[]{:S(2)}) collective-permute-start(bf16[384,256]{0,1:T(8,128)(2,1)S(1)} %collective-permute-done.14), channel_id=1, source_target_pairs={{0,4},{4,8},{8,12},{12,16},{16,20},{20,24},{24,28},{28,32},{32,36}... | collective-permute-start | bytes 589832 | tf_op jit(solution)/shard_map/ppermute | solution.py:15
  112.8 0.7 convolution_bitcast_fusion.7
  113.5 1.0 fusion.4
  114.5 0.7 convolution_bitcast_fusion.5
  115.2 1.0 fusion.8
  116.2 0.7 convolution_bitcast_fusion.3
  116.9 1.0 fusion.12
  118.4 1.0 fusion
  119.5 0.7 fusion.36
  120.2 0.7 fusion.39
  120.9 0.7 fusion.42
  121.6 0.7 fusion.45
  122.3 0.7 convolution_bitcast_fusion.1
  123.0 0.9 fusion.85
  124.0 1.3 convolution_convert_fusion
  125.4 75.8 %all-reduce.2.cloned.1.call-done = bf16[384,1024]{1,0:T(8,128)(2,1)} async-done(((bf16[384,1024]{1,0:T(8,128)(2,1)}), bf16[384,1024]{1,0:T(8,128)(2,1)}) %all-reduce.2.cloned.1.call-update) | async-done | bytes 786448 | tf_op jit(solution)/shard_map/psum | solution.py:75
  201.2 2.5 %convert_add_fusion = (f32[384,1024]{1,0:T(8,128)}, f32[384]{0:T(512)S(1)}) fusion(bf16[384,1024]{1,0:T(8,128)(2,1)S(1)} %all_gather.3, bf16[384,1024]{1,0:T(8,128)(2,1)} %all-reduce.2.cloned.1.call-done), kind=kLoop, calls=%fused_computation.1 | loop fusion | flops 1965696 | bytes 3147264 | tf_op jit(solution)/shard_map/add | solution.py:75
  203.8 7.6 %convolution_convert_fusion.1 = bf16[384,1024]{1,0:T(8,128)(2,1)} fusion(bf16[1024,1024]{1,0:T(8,128)(2,1)S(1)} %copy-done, bf16[1024,1024]{1,0:T(8,128)(2,1)} %param.14, f32[1024]{0:T(1024)S(1)} %copy-done.2, f32[384]{0:T(512)S(1)} %add_rsqrt_fusion, bf16[384,1024]{1,0:T(8,128)(2,1)S(1)} %all_gather.3, bf16[384,1024]{1,0:T(8,128)(2,1)} %all-reduce.2.cloned.1.call-done), kind=kOutput, calls=%fused_computation.65 | convolution fusion | flops 1638924288 | bytes 6559232 | tf_op jit(solution)/shard_map/dot_general | solution.py:80
  211.4 23.1 %reduce-scatter.2.cloned.1.call-done = bf16[384,256]{1,0:T(8,128)(2,1)} async-done(((bf16[384,1024]{1,0:T(8,128)(2,1)}), bf16[384,256]{1,0:T(8,128)(2,1)}) %reduce-scatter.2.cloned.1.call-update) | async-done | bytes 196624 | tf_op jit(solution)/shard_map/reduce_scatter | solution.py:81
  234.5 1.8 add_convert_fusion
  (51 shorter events, 5.9 us)
Async XLA Ops:
  6.5 197.2 %copy-start = (bf16[1024,1024]{1,0:T(8,128)(2,1)S(1)}, bf16[1024,1024]{1,0:T(8,128)(2,1)}, u32[]{:S(2)}) copy-start(bf16[1024,1024]{1,0:T(8,128)(2,1)} %param.15) | copy-start | bytes 6291460
  6.5 194.7 %all-reduce.2.cloned.1.call-start = ((), (), s32[]{:S(2)}) async-start(), calls=%async_computation.1 | async-start | bytes 1572864 | tf_op jit(solution)/shard_map/psum | solution.py:75
  7.4 15.2 %collective-permute-start = (s32[384]{0:T(512)S(1)}, s32[384]{0:T(512)S(1)}, u32[]{:S(2)}, u32[]{:S(2)}) collective-permute-start(s32[384]{0:T(512)S(1)} %broadcast_add_fusion), channel_id=1, source_target_pairs={{0,4},{4,8},{8,12},{12,16},{16,20},{20,24},{24,28},{28,32},{32,36}... | collective-permute-start | bytes 4616 | tf_op jit(solution)/shard_map/ppermute | solution.py:15
  11.4 15.4 %collective-permute-start.3 = (s32[384]{0:T(512)S(1)}, s32[384]{0:T(512)S(1)}, u32[]{:S(2)}, u32[]{:S(2)}) collective-permute-start(s32[384]{0:T(512)S(1)} %broadcast_add_fusion), channel_id=1, source_target_pairs={{4,0},{8,4},{12,8},{16,12},{20,16},{24,20},{28,24},{32,28},{36,32}... | collective-permute-start | bytes 4616 | tf_op jit(solution)/shard_map/ppermute | solution.py:15
  22.5 8.1 %collective-permute-start.6 = (s32[384]{0:T(512)S(1)}, s32[384]{0:T(512)S(1)}, u32[]{:S(2)}, u32[]{:S(2)}) collective-permute-start(s32[384]{0:T(512)S(1)} %collective-permute-done), channel_id=1, source_target_pairs={{0,4},{4,8},{8,12},{12,16},{16,20},{20,24},{24,28},{28,32},{32,36}... | collective-permute-start | bytes 4616 | tf_op jit(solution)/shard_map/ppermute | solution.py:15
  26.8 7.8 %collective-permute-start.9 = (s32[384]{0:T(512)S(1)}, s32[384]{0:T(512)S(1)}, u32[]{:S(2)}, u32[]{:S(2)}) collective-permute-start(s32[384]{0:T(512)S(1)} %collective-permute-done.3), channel_id=1, source_target_pairs={{4,0},{8,4},{12,8},{16,12},{20,16},{24,20},{28,24},{32,28},{36,32}... | collective-permute-start | bytes 4616 | tf_op jit(solution)/shard_map/ppermute | solution.py:15
  30.7 12.0 %collective-permute-start.12 = (s32[384]{0:T(512)S(1)}, s32[384]{0:T(512)S(1)}, u32[]{:S(2)}, u32[]{:S(2)}) collective-permute-start(s32[384]{0:T(512)S(1)} %collective-permute-done.6), channel_id=1, source_target_pairs={{0,4},{4,8},{8,12},{12,16},{16,20},{20,24},{24,28},{28,32},{32,36}... | collective-permute-start | bytes 4616 | tf_op jit(solution)/shard_map/ppermute | solution.py:15
  34.7 16.3 %collective-permute-start.15 = (s32[384]{0:T(512)S(1)}, s32[384]{0:T(512)S(1)}, u32[]{:S(2)}, u32[]{:S(2)}) collective-permute-start(s32[384]{0:T(512)S(1)} %collective-permute-done.9), channel_id=1, source_target_pairs={{4,0},{8,4},{12,8},{16,12},{20,16},{24,20},{28,24},{32,28},{36,32}... | collective-permute-start | bytes 4616 | tf_op jit(solution)/shard_map/ppermute | solution.py:15
  36.0 25.5 %collective-permute-start.1 = (bf16[384,256]{0,1:T(8,128)(2,1)S(1)}, bf16[384,256]{0,1:T(8,128)(2,1)S(1)}, u32[]{:S(2)}, u32[]{:S(2)}) collective-permute-start(bf16[384,256]{0,1:T(8,128)(2,1)S(1)} %bitcast.263), channel_id=1, source_target_pairs={{0,4},{4,8},{8,12},{12,16},{16,20},{20,24},{24,28},{28,32},{32,36}... | collective-permute-start | bytes 589832 | tf_op jit(solution)/shard_map/ppermute | solution.py:15
  40.0 28.5 %collective-permute-start.4 = (bf16[384,256]{0,1:T(8,128)(2,1)S(1)}, bf16[384,256]{0,1:T(8,128)(2,1)S(1)}, u32[]{:S(2)}, u32[]{:S(2)}) collective-permute-start(bf16[384,256]{0,1:T(8,128)(2,1)S(1)} %bitcast.264), channel_id=1, source_target_pairs={{4,0},{8,4},{12,8},{16,12},{20,16},{24,20},{28,24},{32,28},{36,32}... | collective-permute-start | bytes 589832 | tf_op jit(solution)/shard_map/ppermute | solution.py:15
  41.3 28.5 %collective-permute-start.5 = (bf16[384,256]{0,1:T(8,128)(2,1)S(1)}, bf16[384,256]{0,1:T(8,128)(2,1)S(1)}, u32[]{:S(2)}, u32[]{:S(2)}) collective-permute-start(bf16[384,256]{0,1:T(8,128)(2,1)S(1)} %bitcast.274), channel_id=1, source_target_pairs={{4,0},{8,4},{12,8},{16,12},{20,16},{24,20},{28,24},{32,28},{36,32}... | collective-permute-start | bytes 589832 | tf_op jit(solution)/shard_map/ppermute | solution.py:15
  42.6 9.6 %collective-permute-start.18 = (s32[384]{0:T(512)S(1)}, s32[384]{0:T(512)S(1)}, u32[]{:S(2)}, u32[]{:S(2)}) collective-permute-start(s32[384]{0:T(512)S(1)} %collective-permute-done.12), channel_id=1, source_target_pairs={{0,4},{4,8},{8,12},{12,16},{16,20},{20,24},{24,28},{28,32},{32,36}... | collective-permute-start | bytes 4616 | tf_op jit(solution)/shard_map/ppermute | solution.py:15
  50.9 9.0 %collective-permute-start.21 = (s32[384]{0:T(512)S(1)}, s32[384]{0:T(512)S(1)}, u32[]{:S(2)}, u32[]{:S(2)}) collective-permute-start(s32[384]{0:T(512)S(1)} %collective-permute-done.15), channel_id=1, source_target_pairs={{4,0},{8,4},{12,8},{16,12},{20,16},{24,20},{28,24},{32,28},{36,32}... | collective-permute-start | bytes 4616 | tf_op jit(solution)/shard_map/ppermute | solution.py:15
  52.3 19.4 %collective-permute-start.2 = (bf16[384,256]{0,1:T(8,128)(2,1)S(1)}, bf16[384,256]{0,1:T(8,128)(2,1)S(1)}, u32[]{:S(2)}, u32[]{:S(2)}) collective-permute-start(bf16[384,256]{0,1:T(8,128)(2,1)S(1)} %bitcast.275), channel_id=1, source_target_pairs={{0,4},{4,8},{8,12},{12,16},{16,20},{20,24},{24,28},{28,32},{32,36}... | collective-permute-start | bytes 589832 | tf_op jit(solution)/shard_map/ppermute | solution.py:15
  61.5 19.0 %collective-permute-start.7 = (bf16[384,256]{0,1:T(8,128)(2,1)S(1)}, bf16[384,256]{0,1:T(8,128)(2,1)S(1)}, u32[]{:S(2)}, u32[]{:S(2)}) collective-permute-start(bf16[384,256]{0,1:T(8,128)(2,1)S(1)} %collective-permute-done.1), channel_id=1, source_target_pairs={{0,4},{4,8},{8,12},{12,16},{16,20},{20,24},{24,28},{28,32},{32,36}... | collective-permute-start | bytes 589832 | tf_op jit(solution)/shard_map/ppermute | solution.py:15
  68.5 19.0 %collective-permute-start.10 = (bf16[384,256]{0,1:T(8,128)(2,1)S(1)}, bf16[384,256]{0,1:T(8,128)(2,1)S(1)}, u32[]{:S(2)}, u32[]{:S(2)}) collective-permute-start(bf16[384,256]{0,1:T(8,128)(2,1)S(1)} %collective-permute-done.4), channel_id=1, source_target_pairs={{4,0},{8,4},{12,8},{16,12},{20,16},{24,20},{28,24},{32,28},{36,32}... | collective-permute-start | bytes 589832 | tf_op jit(solution)/shard_map/ppermute | solution.py:15
  69.8 19.6 %collective-permute-start.11 = (bf16[384,256]{0,1:T(8,128)(2,1)S(1)}, bf16[384,256]{0,1:T(8,128)(2,1)S(1)}, u32[]{:S(2)}, u32[]{:S(2)}) collective-permute-start(bf16[384,256]{0,1:T(8,128)(2,1)S(1)} %collective-permute-done.5), channel_id=1, source_target_pairs={{4,0},{8,4},{12,8},{16,12},{20,16},{24,20},{28,24},{32,28},{36,32}... | collective-permute-start | bytes 589832 | tf_op jit(solution)/shard_map/ppermute | solution.py:15
  71.7 19.6 %collective-permute-start.8 = (bf16[384,256]{0,1:T(8,128)(2,1)S(1)}, bf16[384,256]{0,1:T(8,128)(2,1)S(1)}, u32[]{:S(2)}, u32[]{:S(2)}) collective-permute-start(bf16[384,256]{0,1:T(8,128)(2,1)S(1)} %collective-permute-done.2), channel_id=1, source_target_pairs={{0,4},{4,8},{8,12},{12,16},{16,20},{20,24},{24,28},{28,32},{32,36}... | collective-permute-start | bytes 589832 | tf_op jit(solution)/shard_map/ppermute | solution.py:15
  80.6 15.4 %collective-permute-start.13 = (bf16[384,256]{0,1:T(8,128)(2,1)S(1)}, bf16[384,256]{0,1:T(8,128)(2,1)S(1)}, u32[]{:S(2)}, u32[]{:S(2)}) collective-permute-start(bf16[384,256]{0,1:T(8,128)(2,1)S(1)} %collective-permute-done.7), channel_id=1, source_target_pairs={{0,4},{4,8},{8,12},{12,16},{16,20},{20,24},{24,28},{28,32},{32,36}... | collective-permute-start | bytes 589832 | tf_op jit(solution)/shard_map/ppermute | solution.py:15
  87.5 15.4 %collective-permute-start.16 = (bf16[384,256]{0,1:T(8,128)(2,1)S(1)}, bf16[384,256]{0,1:T(8,128)(2,1)S(1)}, u32[]{:S(2)}, u32[]{:S(2)}) collective-permute-start(bf16[384,256]{0,1:T(8,128)(2,1)S(1)} %collective-permute-done.10), channel_id=1, source_target_pairs={{4,0},{8,4},{12,8},{16,12},{20,16},{24,20},{28,24},{32,28},{36,32}... | collective-permute-start | bytes 589832 | tf_op jit(solution)/shard_map/ppermute | solution.py:15
  89.4 14.9 %collective-permute-start.17 = (bf16[384,256]{0,1:T(8,128)(2,1)S(1)}, bf16[384,256]{0,1:T(8,128)(2,1)S(1)}, u32[]{:S(2)}, u32[]{:S(2)}) collective-permute-start(bf16[384,256]{0,1:T(8,128)(2,1)S(1)} %collective-permute-done.11), channel_id=1, source_target_pairs={{4,0},{8,4},{12,8},{16,12},{20,16},{24,20},{28,24},{32,28},{36,32}... | collective-permute-start | bytes 589832 | tf_op jit(solution)/shard_map/ppermute | solution.py:15
  91.3 14.9 %collective-permute-start.14 = (bf16[384,256]{0,1:T(8,128)(2,1)S(1)}, bf16[384,256]{0,1:T(8,128)(2,1)S(1)}, u32[]{:S(2)}, u32[]{:S(2)}) collective-permute-start(bf16[384,256]{0,1:T(8,128)(2,1)S(1)} %collective-permute-done.8), channel_id=1, source_target_pairs={{0,4},{4,8},{8,12},{12,16},{16,20},{20,24},{24,28},{28,32},{32,36}... | collective-permute-start | bytes 589832 | tf_op jit(solution)/shard_map/ppermute | solution.py:15
  96.0 15.6 %collective-permute-start.19 = (bf16[384,256]{0,1:T(8,128)(2,1)S(1)}, bf16[384,256]{0,1:T(8,128)(2,1)S(1)}, u32[]{:S(2)}, u32[]{:S(2)}) collective-permute-start(bf16[384,256]{0,1:T(8,128)(2,1)S(1)} %collective-permute-done.13), channel_id=1, source_target_pairs={{0,4},{4,8},{8,12},{12,16},{16,20},{20,24},{24,28},{28,32},{32,36}... | collective-permute-start | bytes 589832 | tf_op jit(solution)/shard_map/ppermute | solution.py:15
  103.0 9.2 %collective-permute-start.22 = (bf16[384,256]{0,1:T(8,128)(2,1)S(1)}, bf16[384,256]{0,1:T(8,128)(2,1)S(1)}, u32[]{:S(2)}, u32[]{:S(2)}) collective-permute-start(bf16[384,256]{0,1:T(8,128)(2,1)S(1)} %collective-permute-done.16), channel_id=1, source_target_pairs={{4,0},{8,4},{12,8},{16,12},{20,16},{24,20},{28,24},{32,28},{36,32}... | collective-permute-start | bytes 589832 | tf_op jit(solution)/shard_map/ppermute | solution.py:15
  104.3 18.0 %collective-permute-start.23 = (bf16[384,256]{0,1:T(8,128)(2,1)S(1)}, bf16[384,256]{0,1:T(8,128)(2,1)S(1)}, u32[]{:S(2)}, u32[]{:S(2)}) collective-permute-start(bf16[384,256]{0,1:T(8,128)(2,1)S(1)} %collective-permute-done.17), channel_id=1, source_target_pairs={{4,0},{8,4},{12,8},{16,12},{20,16},{24,20},{28,24},{32,28},{36,32}... | collective-permute-start | bytes 589832 | tf_op jit(solution)/shard_map/ppermute | solution.py:15
  106.2 16.8 %collective-permute-start.20 = (bf16[384,256]{0,1:T(8,128)(2,1)S(1)}, bf16[384,256]{0,1:T(8,128)(2,1)S(1)}, u32[]{:S(2)}, u32[]{:S(2)}) collective-permute-start(bf16[384,256]{0,1:T(8,128)(2,1)S(1)} %collective-permute-done.14), channel_id=1, source_target_pairs={{0,4},{4,8},{8,12},{12,16},{16,20},{20,24},{24,28},{28,32},{32,36}... | collective-permute-start | bytes 589832 | tf_op jit(solution)/shard_map/ppermute | solution.py:15
  123.0 1.0 copy-start.1
  124.0 79.7 %copy-start.2 = (f32[1024]{0:T(1024)S(1)}, f32[1024]{0:T(1024)}, u32[]{:S(2)}) copy-start(f32[1024]{0:T(1024)} %param.13) | copy-start | bytes 12292
  125.3 109.1 %reduce-scatter.2.cloned.1.call-start = ((), (), s32[]{:S(2)}) async-start(), calls=%async_computation.2 | async-start | bytes 983040 | tf_op jit(solution)/shard_map/reduce_scatter | solution.py:81
Sparse Core Ops, SparseCore 0:
  125.4 75.7 all-reduce.1
  211.5 22.8 reduce-scatter.1
where the time goes:
time: 244 us; the launch traced here: 243 us
  waiting for transfers between devices  99 us (41%)
  starting transfers between devices  86.3 us (35%)
  matrix products  22.9 us (9%)
  between operations  13.9 us (6%)
  other arithmetic  11.2 us (5%)
  blocking collectives  9.6 us (4%)
    ppermute x24, starting transfers between devices, shifted(): return lax.ppermute(block, axis, route)  86.2 us
    psum x1, waiting for transfers between devices, shards(): lax.psum(attn_part.astype(jnp.bfloat16), 'tp').astype(jnp.float32)  75.8 us
    reduce_scatter x1, waiting for transfers between devices, shards(): lax.psum_scatter(ffn_part.astype(jnp.bfloat16), 'tp', scatter_dimension=1...  23.1 us
    all_gather x1, blocking collectives, shards(): lax.all_gather(hit_features, 'tp', axis=1, tiled=True).astype(jnp.float32)  9.6 us
    dot_general x1, matrix products, shards(): ffn_part = jnp.dot(hidden, w_down, preferred_element_type=jnp.float32)  7.62 us
    dot_general x9, matrix products, absorb(): jnp.einsum('hqk,khd->hqd', powered.astype(jnp.bfloat16), value_heads, pre...  6.29 us
    dot_general x9, matrix products, absorb(): jnp.einsum('qhd,khd->hqk', query_heads, key_heads, preferred_element_type...  5.23 us
  transfers between devices with their start and end apart: 26, of which 2 were waited for; matrix products, arithmetic and copies ran while one was open for 8% of the time, Pallas kernels for 0%

commit v1 on v0

--- a/solution.py
+++ b/solution.py
@@ -42,7 +42,9 @@
 
 
 def shards(hit_features, segment, norm1_gain, w_qkv, w_out, norm2_gain, w_up, w_down):
-    features = lax.all_gather(hit_features, "tp", axis=1, tiled=True).astype(jnp.float32)
+    features = jnp.concatenate(
+        lax.all_to_all(jnp.stack([hit_features] * lax.axis_size("tp")), "tp", 0, 0), axis=1
+    ).astype(jnp.float32)
     normed = rms_scale(features, norm1_gain).astype(jnp.bfloat16)
     projected = jnp.einsum("td,cde->cte", normed, w_qkv, preferred_element_type=jnp.float32)
     queries = (projected[0] * HEAD_DIM ** (-0.5)).astype(jnp.bfloat16)

time: 244 us -> 252 us (1.033)
  blocking collectives: 9.6 us -> 0 us
  waiting for transfers between devices: 99 us -> 107 us
  starting transfers between devices: 86.3 us -> 92.6 us
  local copies, waits for them, and re-layouts: 0.2 us -> 3.95 us
    all_gather x1 -> x0, blocking collectives: 9.6 us -> none  [shards(): lax.all_gather(hit_features, 'tp', axis=1, tiled=True).astype(jnp.float32)]
    ppermute x24, waiting for transfers between devices: 0.06 us -> 7.09 us  [shifted(): return lax.ppermute(block, axis, route)]
    all_to_all x0 -> x1, starting transfers between devices: none -> 6.66 us  [shards(): lax.all_to_all(jnp.stack([hit_features] * lax.axis_size('tp')), 'tp', 0, 0)]
    reduce_sum x1 -> x2, other arithmetic: 0.23 us -> 3.19 us  [rms_scale(): mean_square = jnp.mean(features * features, axis=-1, keepdims=True)]
    add x1 -> x0, other arithmetic: 2.53 us -> none  [shards(): features + lax.psum(attn_part.astype(jnp.bfloat16), 'tp').astype(jnp.floa...]
  transfers between devices with their start and end apart: 26 -> 27, of which waited for: 2 -> 3; matrix products, arithmetic and copies ran while one was open for 8% -> 7% of each run, Pallas kernels for 0% -> 0%
where the time goes in v1:
time: 252 us; the launch traced here: 251 us
  waiting for transfers between devices  107 us (42%)
  starting transfers between devices  92.6 us (37%)
  matrix products  21.7 us (9%)
  between operations  14.1 us (6%)
  other arithmetic  11.8 us (5%)
  local copies, waits for them, and re-layouts  3.95 us (2%)
    ppermute x24, starting transfers between devices, shifted(): return lax.ppermute(block, axis, route)  85.9 us
    psum x1, waiting for transfers between devices, shards(): lax.psum(attn_part.astype(jnp.bfloat16), 'tp').astype(jnp.float32)  77.3 us
    reduce_scatter x1, waiting for transfers between devices, shards(): lax.psum_scatter(ffn_part.astype(jnp.bfloat16), 'tp', scatter_dimension=1...  23.1 us
    dot_general x1, matrix products, shards(): ffn_part = jnp.dot(hidden, w_down, preferred_element_type=jnp.float32)  7.82 us
    ppermute x24, waiting for transfers between devices, shifted(): return lax.ppermute(block, axis, route)  7.09 us
    all_to_all x1, starting transfers between devices, shards(): lax.all_to_all(jnp.stack([hit_features] * lax.axis_size('tp')), 'tp', 0, 0)  6.66 us
    dot_general x9, matrix products, absorb(): jnp.einsum('hqk,khd->hqd', powered.astype(jnp.bfloat16), value_heads, pre...  6.26 us
    dot_general x9, matrix products, absorb(): jnp.einsum('qhd,khd->hqk', query_heads, key_heads, preferred_element_type...  5.2 us
  transfers between devices with their start and end apart: 27, of which 3 were waited for; matrix products, arithmetic and copies ran while one was open for 7% of the time, Pallas kernels for 0%

profile of v1, /device:TPU:1, one launch (start us, length us, event | category | flops | bytes accessed | tf_op | source)
XLA Modules:
  0.0 251.4 jit_solution(17344244168852457251)
XLA Ops:
  6.5 2.0 stack.2
  8.6 6.7 %all-to-all-start = ((bf16[4,384,256]{2,1,0:T(8,128)(2,1)}), bf16[4,384,256]{2,1,0:T(8,128)(2,1)S(1)}, u32[]{:S(2)}, u32[]{:S(2)}) async-start(bf16[4,384,256]{2,1,0:T(8,128)(2,1)} %stack.2), calls=%async_computation | async-start | bytes 1572864 | tf_op jit(solution)/shard_map/all_to_all | solution.py:46
  15.2 1.5 collective-permute-start
  16.7 1.3 collective-permute-start.3
  18.0 4.0 %collective-permute-start.6 = (s32[384]{0:T(512)S(1)}, s32[384]{0:T(512)S(1)}, u32[]{:S(2)}, u32[]{:S(2)}) collective-permute-start(s32[384]{0:T(512)S(1)} %collective-permute-done), channel_id=1, source_target_pairs={{0,4},{4,8},{8,12},{12,16},{16,20},{20,24},{24,28},{28,32},{32,36}... | collective-permute-start | bytes 4616 | tf_op jit(solution)/shard_map/ppermute | solution.py:15
  22.0 1.3 collective-permute-start.9
  23.4 4.0 %collective-permute-start.12 = (s32[384]{0:T(512)S(1)}, s32[384]{0:T(512)S(1)}, u32[]{:S(2)}, u32[]{:S(2)}) collective-permute-start(s32[384]{0:T(512)S(1)} %collective-permute-done.6), channel_id=1, source_target_pairs={{0,4},{4,8},{8,12},{12,16},{16,20},{20,24},{24,28},{28,32},{32,36}... | collective-permute-start | bytes 4616 | tf_op jit(solution)/shard_map/ppermute | solution.py:15
  27.4 1.3 collective-permute-start.15
  28.7 7.1 %collective-permute-start.18 = (s32[384]{0:T(512)S(1)}, s32[384]{0:T(512)S(1)}, u32[]{:S(2)}, u32[]{:S(2)}) collective-permute-start(s32[384]{0:T(512)S(1)} %collective-permute-done.12), channel_id=1, source_target_pairs={{0,4},{4,8},{8,12},{12,16},{16,20},{20,24},{24,28},{28,32},{32,36}... | collective-permute-start | bytes 4616 | tf_op jit(solution)/shard_map/ppermute | solution.py:15
  35.8 1.3 collective-permute-start.21
  37.1 7.0 %collective-permute-done.21 = s32[384]{0:T(512)S(1)} collective-permute-done((s32[384]{0:T(512)S(1)}, s32[384]{0:T(512)S(1)}, u32[]{:S(2)}, u32[]{:S(2)}) %collective-permute-start.21) | collective-permute-done | bytes 1568 | tf_op jit(solution)/shard_map/ppermute | solution.py:15
  44.1 1.9 broadcast_compare_fusion.8
  46.6 1.5 copy-done.2
  48.1 1.1 convolution_bitcast_fusion
  49.3 7.0 %collective-permute-start.1 = (bf16[384,256]{0,1:T(8,128)(2,1)S(1)}, bf16[384,256]{0,1:T(8,128)(2,1)S(1)}, u32[]{:S(2)}, u32[]{:S(2)}) collective-permute-start(bf16[384,256]{0,1:T(8,128)(2,1)S(1)} %bitcast.269), channel_id=1, source_target_pairs={{0,4},{4,8},{8,12},{12,16},{16,20},{20,24},{24,28},{28,32},{32,36}... | collective-permute-start | bytes 589832 | tf_op jit(solution)/shard_map/ppermute | solution.py:15
  56.3 1.3 collective-permute-start.4
  57.6 1.3 collective-permute-start.5
  58.9 8.2 %collective-permute-start.2 = (bf16[384,256]{0,1:T(8,128)(2,1)S(1)}, bf16[384,256]{0,1:T(8,128)(2,1)S(1)}, u32[]{:S(2)}, u32[]{:S(2)}) collective-permute-start(bf16[384,256]{0,1:T(8,128)(2,1)S(1)} %bitcast.281), channel_id=1, source_target_pairs={{0,4},{4,8},{8,12},{12,16},{16,20},{20,24},{24,28},{28,32},{32,36}... | collective-permute-start | bytes 589832 | tf_op jit(solution)/shard_map/ppermute | solution.py:15
  67.8 7.0 %collective-permute-start.7 = (bf16[384,256]{0,1:T(8,128)(2,1)S(1)}, bf16[384,256]{0,1:T(8,128)(2,1)S(1)}, u32[]{:S(2)}, u32[]{:S(2)}) collective-permute-start(bf16[384,256]{0,1:T(8,128)(2,1)S(1)} %collective-permute-done.1), channel_id=1, source_target_pairs={{0,4},{4,8},{8,12},{12,16},{16,20},{20,24},{24,28},{28,32},{32,36}... | collective-permute-start | bytes 589832 | tf_op jit(solution)/shard_map/ppermute | solution.py:15
  74.8 1.3 collective-permute-start.10
  76.1 1.3 collective-permute-start.11
  78.0 4.6 %collective-permute-start.8 = (bf16[384,256]{0,1:T(8,128)(2,1)S(1)}, bf16[384,256]{0,1:T(8,128)(2,1)S(1)}, u32[]{:S(2)}, u32[]{:S(2)}) collective-permute-start(bf16[384,256]{0,1:T(8,128)(2,1)S(1)} %collective-permute-done.2), channel_id=1, source_target_pairs={{0,4},{4,8},{8,12},{12,16},{16,20},{20,24},{24,28},{28,32},{32,36}... | collective-permute-start | bytes 589832 | tf_op jit(solution)/shard_map/ppermute | solution.py:15
  83.2 1.3 collective-permute-start.16
  84.6 7.6 %collective-permute-start.13 = (bf16[384,256]{0,1:T(8,128)(2,1)S(1)}, bf16[384,256]{0,1:T(8,128)(2,1)S(1)}, u32[]{:S(2)}, u32[]{:S(2)}) collective-permute-start(bf16[384,256]{0,1:T(8,128)(2,1)S(1)} %collective-permute-done.7), channel_id=1, source_target_pairs={{0,4},{4,8},{8,12},{12,16},{16,20},{20,24},{24,28},{28,32},{32,36}... | collective-permute-start | bytes 589832 | tf_op jit(solution)/shard_map/ppermute | solution.py:15
  92.8 1.3 collective-permute-start.17
  94.7 4.0 %collective-permute-start.14 = (bf16[384,256]{0,1:T(8,128)(2,1)S(1)}, bf16[384,256]{0,1:T(8,128)(2,1)S(1)}, u32[]{:S(2)}, u32[]{:S(2)}) collective-permute-start(bf16[384,256]{0,1:T(8,128)(2,1)S(1)} %collective-permute-done.8), channel_id=1, source_target_pairs={{0,4},{4,8},{8,12},{12,16},{16,20},{20,24},{24,28},{28,32},{32,36}... | collective-permute-start | bytes 589832 | tf_op jit(solution)/shard_map/ppermute | solution.py:15
  98.7 7.0 %collective-permute-start.19 = (bf16[384,256]{0,1:T(8,128)(2,1)S(1)}, bf16[384,256]{0,1:T(8,128)(2,1)S(1)}, u32[]{:S(2)}, u32[]{:S(2)}) collective-permute-start(bf16[384,256]{0,1:T(8,128)(2,1)S(1)} %collective-permute-done.13), channel_id=1, source_target_pairs={{0,4},{4,8},{8,12},{12,16},{16,20},{20,24},{24,28},{28,32},{32,36}... | collective-permute-start | bytes 589832 | tf_op jit(solution)/shard_map/ppermute | solution.py:15
  105.7 1.3 collective-permute-start.22
  107.0 1.3 collective-permute-start.23
  108.9 8.4 %collective-permute-start.20 = (bf16[384,256]{0,1:T(8,128)(2,1)S(1)}, bf16[384,256]{0,1:T(8,128)(2,1)S(1)}, u32[]{:S(2)}, u32[]{:S(2)}) collective-permute-start(bf16[384,256]{0,1:T(8,128)(2,1)S(1)} %collective-permute-done.14), channel_id=1, source_target_pairs={{0,4},{4,8},{8,12},{12,16},{16,20},{20,24},{24,28},{28,32},{32,36}... | collective-permute-start | bytes 589832 | tf_op jit(solution)/shard_map/ppermute | solution.py:15
  119.1 0.7 convolution_bitcast_fusion.7
  119.8 1.0 fusion.4
  121.5 1.0 fusion.8
  122.5 0.7 convolution_bitcast_fusion.3
  123.2 1.0 fusion.12
  124.7 1.0 fusion
  125.8 0.7 fusion.34
  126.5 0.7 fusion.37
  127.1 0.7 fusion.40
  127.8 0.7 fusion.43
  128.6 0.7 convolution_bitcast_fusion.1
  129.2 0.9 fusion.83
  130.3 1.3 convolution_convert_fusion
  131.6 77.3 %all-reduce.2.cloned.1.call-done = bf16[384,1024]{1,0:T(8,128)(2,1)} async-done(((bf16[384,1024]{1,0:T(8,128)(2,1)}), bf16[384,1024]{1,0:T(8,128)(2,1)}) %all-reduce.2.cloned.1.call-update) | async-done | bytes 786448 | tf_op jit(solution)/shard_map/psum | solution.py:77
  208.9 3.0 %multiply_reduce_fusion = (f32[384]{0:T(512)S(1)}, f32[384,1024]{1,0:T(8,128)}) fusion(f32[384,1024]{1,0:T(8,128)} %bitcast.268, bf16[384,1024]{1,0:T(8,128)(2,1)} %all-reduce.2.cloned.1.call-done), kind=kLoop, calls=%fused_computation.57 | loop fusion | flops 1572480 | bytes 3933696 | tf_op jit(solution)/shard_map/reduce_sum | solution.py:19
  211.9 7.8 %convolution_convert_fusion.1 = bf16[384,1024]{1,0:T(8,128)(2,1)} fusion(bf16[1024,1024]{1,0:T(8,128)(2,1)S(1)} %copy-done, bf16[1024,1024]{1,0:T(8,128)(2,1)} %param.14, f32[384,1024]{1,0:T(8,128)} %get-tuple-element.6, f32[1024]{0:T(1024)S(1)} %copy-done.11, f32[384]{0:T(512)S(1)} %add_rsqrt_fusion), kind=kOutput, calls=%fused_computation.64 | convolution fusion | flops 1637744640 | bytes 6559232 | tf_op jit(solution)/shard_map/dot_general | solution.py:82
  219.7 23.1 %reduce-scatter.2.cloned.1.call-done = bf16[384,256]{1,0:T(8,128)(2,1)} async-done(((bf16[384,1024]{1,0:T(8,128)(2,1)}), bf16[384,256]{1,0:T(8,128)(2,1)}) %reduce-scatter.2.cloned.1.call-update) | async-done | bytes 196624 | tf_op jit(solution)/shard_map/reduce_scatter | solution.py:83
  242.8 1.8 add_convert_fusion
  (73 shorter events, 7.4 us)
Async XLA Ops:
  6.5 205.3 %copy-start = (bf16[1024,1024]{1,0:T(8,128)(2,1)S(1)}, bf16[1024,1024]{1,0:T(8,128)(2,1)}, u32[]{:S(2)}) copy-start(bf16[1024,1024]{1,0:T(8,128)(2,1)} %param.15) | copy-start | bytes 6291460
  6.5 8.7 %copy-start.10 = (s32[384]{0:T(512)S(1)}, s32[384]{0:T(512)}, u32[]{:S(2)}) copy-start(s32[384]{0:T(512)} %param.9) | copy-start | bytes 4612
  8.6 37.5 %all-to-all-start = ((bf16[4,384,256]{2,1,0:T(8,128)(2,1)}), bf16[4,384,256]{2,1,0:T(8,128)(2,1)S(1)}, u32[]{:S(2)}, u32[]{:S(2)}) async-start(bf16[4,384,256]{2,1,0:T(8,128)(2,1)} %stack.2), calls=%async_computation | async-start | bytes 1572864 | tf_op jit(solution)/shard_map/all_to_all | solution.py:46
  15.2 193.7 %all-reduce.2.cloned.1.call-start = ((), (), s32[]{:S(2)}) async-start(), calls=%async_computation.2 | async-start | bytes 1572864 | tf_op jit(solution)/shard_map/psum | solution.py:77
  15.2 2.8 %collective-permute-start = (s32[384]{0:T(512)S(1)}, s32[384]{0:T(512)S(1)}, u32[]{:S(2)}, u32[]{:S(2)}) collective-permute-start(s32[384]{0:T(512)S(1)} %broadcast_add_fusion), channel_id=1, source_target_pairs={{0,4},{4,8},{8,12},{12,16},{16,20},{20,24},{24,28},{28,32},{32,36}... | collective-permute-start | bytes 4616 | tf_op jit(solution)/shard_map/ppermute | solution.py:15
  16.7 5.3 %collective-permute-start.3 = (s32[384]{0:T(512)S(1)}, s32[384]{0:T(512)S(1)}, u32[]{:S(2)}, u32[]{:S(2)}) collective-permute-start(s32[384]{0:T(512)S(1)} %broadcast_add_fusion), channel_id=1, source_target_pairs={{4,0},{8,4},{12,8},{16,12},{20,16},{24,20},{28,24},{32,28},{36,32}... | collective-permute-start | bytes 4616 | tf_op jit(solution)/shard_map/ppermute | solution.py:15
  18.0 5.3 %collective-permute-start.6 = (s32[384]{0:T(512)S(1)}, s32[384]{0:T(512)S(1)}, u32[]{:S(2)}, u32[]{:S(2)}) collective-permute-start(s32[384]{0:T(512)S(1)} %collective-permute-done), channel_id=1, source_target_pairs={{0,4},{4,8},{8,12},{12,16},{16,20},{20,24},{24,28},{28,32},{32,36}... | collective-permute-start | bytes 4616 | tf_op jit(solution)/shard_map/ppermute | solution.py:15
  22.0 5.3 %collective-permute-start.9 = (s32[384]{0:T(512)S(1)}, s32[384]{0:T(512)S(1)}, u32[]{:S(2)}, u32[]{:S(2)}) collective-permute-start(s32[384]{0:T(512)S(1)} %collective-permute-done.3), channel_id=1, source_target_pairs={{4,0},{8,4},{12,8},{16,12},{20,16},{24,20},{28,24},{32,28},{36,32}... | collective-permute-start | bytes 4616 | tf_op jit(solution)/shard_map/ppermute | solution.py:15
  23.4 5.3 %collective-permute-start.12 = (s32[384]{0:T(512)S(1)}, s32[384]{0:T(512)S(1)}, u32[]{:S(2)}, u32[]{:S(2)}) collective-permute-start(s32[384]{0:T(512)S(1)} %collective-permute-done.6), channel_id=1, source_target_pairs={{0,4},{4,8},{8,12},{12,16},{16,20},{20,24},{24,28},{28,32},{32,36}... | collective-permute-start | bytes 4616 | tf_op jit(solution)/shard_map/ppermute | solution.py:15
  27.4 8.4 %collective-permute-start.15 = (s32[384]{0:T(512)S(1)}, s32[384]{0:T(512)S(1)}, u32[]{:S(2)}, u32[]{:S(2)}) collective-permute-start(s32[384]{0:T(512)S(1)} %collective-permute-done.9), channel_id=1, source_target_pairs={{4,0},{8,4},{12,8},{16,12},{20,16},{24,20},{28,24},{32,28},{36,32}... | collective-permute-start | bytes 4616 | tf_op jit(solution)/shard_map/ppermute | solution.py:15
  28.7 8.4 %collective-permute-start.18 = (s32[384]{0:T(512)S(1)}, s32[384]{0:T(512)S(1)}, u32[]{:S(2)}, u32[]{:S(2)}) collective-permute-start(s32[384]{0:T(512)S(1)} %collective-permute-done.12), channel_id=1, source_target_pairs={{0,4},{4,8},{8,12},{12,16},{16,20},{20,24},{24,28},{28,32},{32,36}... | collective-permute-start | bytes 4616 | tf_op jit(solution)/shard_map/ppermute | solution.py:15
  35.8 8.3 %collective-permute-start.21 = (s32[384]{0:T(512)S(1)}, s32[384]{0:T(512)S(1)}, u32[]{:S(2)}, u32[]{:S(2)}) collective-permute-start(s32[384]{0:T(512)S(1)} %collective-permute-done.15), channel_id=1, source_target_pairs={{4,0},{8,4},{12,8},{16,12},{20,16},{24,20},{28,24},{32,28},{36,32}... | collective-permute-start | bytes 4616 | tf_op jit(solution)/shard_map/ppermute | solution.py:15
  46.1 2.0 copy-start.2
  46.2 2.0 copy-start.9
  46.4 2.9 %copy-start.1 = (f32[4,48,8,256]{3,2,0,1:T(8,128)}, f32[4,48,8,256]{3,2,0,1:T(8,128)S(1)}, u32[]{:S(2)}) copy-start(f32[4,48,8,256]{3,2,0,1:T(8,128)S(1)} %copy.40) | copy-start | bytes 4718596
  48.1 19.1 %copy-start.4 = (pred[384,384]{0,1:T(8,128)(4,1)S(1)}, pred[384,384]{0,1:T(8,128)(4,1)}, u32[]{:S(2)}) copy-start(pred[384,384]{0,1:T(8,128)(4,1)} %get-tuple-element.30) | copy-start | bytes 442372
  49.2 28.2 %copy-start.3 = (pred[384,384]{0,1:T(8,128)(4,1)S(1)}, pred[384,384]{0,1:T(8,128)(4,1)}, u32[]{:S(2)}) copy-start(pred[384,384]{0,1:T(8,128)(4,1)} %get-tuple-element.38) | copy-start | bytes 442372
  49.3 18.4 %collective-permute-start.1 = (bf16[384,256]{0,1:T(8,128)(2,1)S(1)}, bf16[384,256]{0,1:T(8,128)(2,1)S(1)}, u32[]{:S(2)}, u32[]{:S(2)}) collective-permute-start(bf16[384,256]{0,1:T(8,128)(2,1)S(1)} %bitcast.269), channel_id=1, source_target_pairs={{0,4},{4,8},{8,12},{12,16},{16,20},{20,24},{24,28},{28,32},{32,36}... | collective-permute-start | bytes 589832 | tf_op jit(solution)/shard_map/ppermute | solution.py:15
  56.3 18.4 %collective-permute-start.4 = (bf16[384,256]{0,1:T(8,128)(2,1)S(1)}, bf16[384,256]{0,1:T(8,128)(2,1)S(1)}, u32[]{:S(2)}, u32[]{:S(2)}) collective-permute-start(bf16[384,256]{0,1:T(8,128)(2,1)S(1)} %bitcast.270), channel_id=1, source_target_pairs={{4,0},{8,4},{12,8},{16,12},{20,16},{24,20},{28,24},{32,28},{36,32}... | collective-permute-start | bytes 589832 | tf_op jit(solution)/shard_map/ppermute | solution.py:15
  57.6 18.4 %collective-permute-start.5 = (bf16[384,256]{0,1:T(8,128)(2,1)S(1)}, bf16[384,256]{0,1:T(8,128)(2,1)S(1)}, u32[]{:S(2)}, u32[]{:S(2)}) collective-permute-start(bf16[384,256]{0,1:T(8,128)(2,1)S(1)} %bitcast.280), channel_id=1, source_target_pairs={{4,0},{8,4},{12,8},{16,12},{20,16},{24,20},{28,24},{32,28},{36,32}... | collective-permute-start | bytes 589832 | tf_op jit(solution)/shard_map/ppermute | solution.py:15
  58.9 19.0 %collective-permute-start.2 = (bf16[384,256]{0,1:T(8,128)(2,1)S(1)}, bf16[384,256]{0,1:T(8,128)(2,1)S(1)}, u32[]{:S(2)}, u32[]{:S(2)}) collective-permute-start(bf16[384,256]{0,1:T(8,128)(2,1)S(1)} %bitcast.281), channel_id=1, source_target_pairs={{0,4},{4,8},{8,12},{12,16},{16,20},{20,24},{24,28},{28,32},{32,36}... | collective-permute-start | bytes 589832 | tf_op jit(solution)/shard_map/ppermute | solution.py:15
  67.2 15.4 %copy-start.7 = (pred[384,384]{0,1:T(8,128)(4,1)S(1)}, pred[384,384]{0,1:T(8,128)(4,1)}, u32[]{:S(2)}) copy-start(pred[384,384]{0,1:T(8,128)(4,1)} %get-tuple-element.31) | copy-start | bytes 442372
  67.8 16.8 %collective-permute-start.7 = (bf16[384,256]{0,1:T(8,128)(2,1)S(1)}, bf16[384,256]{0,1:T(8,128)(2,1)S(1)}, u32[]{:S(2)}, u32[]{:S(2)}) collective-permute-start(bf16[384,256]{0,1:T(8,128)(2,1)S(1)} %collective-permute-done.1), channel_id=1, source_target_pairs={{0,4},{4,8},{8,12},{12,16},{16,20},{20,24},{24,28},{28,32},{32,36}... | collective-permute-start | bytes 589832 | tf_op jit(solution)/shard_map/ppermute | solution.py:15
  74.8 8.5 %collective-permute-start.10 = (bf16[384,256]{0,1:T(8,128)(2,1)S(1)}, bf16[384,256]{0,1:T(8,128)(2,1)S(1)}, u32[]{:S(2)}, u32[]{:S(2)}) collective-permute-start(bf16[384,256]{0,1:T(8,128)(2,1)S(1)} %collective-permute-done.4), channel_id=1, source_target_pairs={{4,0},{8,4},{12,8},{16,12},{20,16},{24,20},{28,24},{32,28},{36,32}... | collective-permute-start | bytes 589832 | tf_op jit(solution)/shard_map/ppermute | solution.py:15
  76.1 16.7 %collective-permute-start.11 = (bf16[384,256]{0,1:T(8,128)(2,1)S(1)}, bf16[384,256]{0,1:T(8,128)(2,1)S(1)}, u32[]{:S(2)}, u32[]{:S(2)}) collective-permute-start(bf16[384,256]{0,1:T(8,128)(2,1)S(1)} %collective-permute-done.5), channel_id=1, source_target_pairs={{4,0},{8,4},{12,8},{16,12},{20,16},{24,20},{28,24},{32,28},{36,32}... | collective-permute-start | bytes 589832 | tf_op jit(solution)/shard_map/ppermute | solution.py:15
  78.0 16.7 %collective-permute-start.8 = (bf16[384,256]{0,1:T(8,128)(2,1)S(1)}, bf16[384,256]{0,1:T(8,128)(2,1)S(1)}, u32[]{:S(2)}, u32[]{:S(2)}) collective-permute-start(bf16[384,256]{0,1:T(8,128)(2,1)S(1)} %collective-permute-done.2), channel_id=1, source_target_pairs={{0,4},{4,8},{8,12},{12,16},{16,20},{20,24},{24,28},{28,32},{32,36}... | collective-permute-start | bytes 589832 | tf_op jit(solution)/shard_map/ppermute | solution.py:15
  82.6 11.4 %copy-start.6 = (pred[384,384]{0,1:T(8,128)(4,1)S(1)}, pred[384,384]{0,1:T(8,128)(4,1)}, u32[]{:S(2)}) copy-start(pred[384,384]{0,1:T(8,128)(4,1)} %get-tuple-element.33) | copy-start | bytes 442372
  83.2 22.4 %collective-permute-start.16 = (bf16[384,256]{0,1:T(8,128)(2,1)S(1)}, bf16[384,256]{0,1:T(8,128)(2,1)S(1)}, u32[]{:S(2)}, u32[]{:S(2)}) collective-permute-start(bf16[384,256]{0,1:T(8,128)(2,1)S(1)} %collective-permute-done.10), channel_id=1, source_target_pairs={{4,0},{8,4},{12,8},{16,12},{20,16},{24,20},{28,24},{32,28},{36,32}... | collective-permute-start | bytes 589832 | tf_op jit(solution)/shard_map/ppermute | solution.py:15
  84.6 14.1 %collective-permute-start.13 = (bf16[384,256]{0,1:T(8,128)(2,1)S(1)}, bf16[384,256]{0,1:T(8,128)(2,1)S(1)}, u32[]{:S(2)}, u32[]{:S(2)}) collective-permute-start(bf16[384,256]{0,1:T(8,128)(2,1)S(1)} %collective-permute-done.7), channel_id=1, source_target_pairs={{0,4},{4,8},{8,12},{12,16},{16,20},{20,24},{24,28},{28,32},{32,36}... | collective-permute-start | bytes 589832 | tf_op jit(solution)/shard_map/ppermute | solution.py:15
  92.2 16.1 %copy-start.5 = (pred[384,384]{0,1:T(8,128)(4,1)S(1)}, pred[384,384]{0,1:T(8,128)(4,1)}, u32[]{:S(2)}) copy-start(pred[384,384]{0,1:T(8,128)(4,1)} %get-tuple-element.35) | copy-start | bytes 442372
  92.8 14.2 %collective-permute-start.17 = (bf16[384,256]{0,1:T(8,128)(2,1)S(1)}, bf16[384,256]{0,1:T(8,128)(2,1)S(1)}, u32[]{:S(2)}, u32[]{:S(2)}) collective-permute-start(bf16[384,256]{0,1:T(8,128)(2,1)S(1)} %collective-permute-done.11), channel_id=1, source_target_pairs={{4,0},{8,4},{12,8},{16,12},{20,16},{24,20},{28,24},{32,28},{36,32}... | collective-permute-start | bytes 589832 | tf_op jit(solution)/shard_map/ppermute | solution.py:15
  94.7 14.2 %collective-permute-start.14 = (bf16[384,256]{0,1:T(8,128)(2,1)S(1)}, bf16[384,256]{0,1:T(8,128)(2,1)S(1)}, u32[]{:S(2)}, u32[]{:S(2)}) collective-permute-start(bf16[384,256]{0,1:T(8,128)(2,1)S(1)} %collective-permute-done.8), channel_id=1, source_target_pairs={{0,4},{4,8},{8,12},{12,16},{16,20},{20,24},{24,28},{28,32},{32,36}... | collective-permute-start | bytes 589832 | tf_op jit(solution)/shard_map/ppermute | solution.py:15
  98.7 19.2 %collective-permute-start.19 = (bf16[384,256]{0,1:T(8,128)(2,1)S(1)}, bf16[384,256]{0,1:T(8,128)(2,1)S(1)}, u32[]{:S(2)}, u32[]{:S(2)}) collective-permute-start(bf16[384,256]{0,1:T(8,128)(2,1)S(1)} %collective-permute-done.13), channel_id=1, source_target_pairs={{0,4},{4,8},{8,12},{12,16},{16,20},{20,24},{24,28},{28,32},{32,36}... | collective-permute-start | bytes 589832 | tf_op jit(solution)/shard_map/ppermute | solution.py:15
  105.7 12.8 %collective-permute-start.22 = (bf16[384,256]{0,1:T(8,128)(2,1)S(1)}, bf16[384,256]{0,1:T(8,128)(2,1)S(1)}, u32[]{:S(2)}, u32[]{:S(2)}) collective-permute-start(bf16[384,256]{0,1:T(8,128)(2,1)S(1)} %collective-permute-done.16), channel_id=1, source_target_pairs={{4,0},{8,4},{12,8},{16,12},{20,16},{24,20},{28,24},{32,28},{36,32}... | collective-permute-start | bytes 589832 | tf_op jit(solution)/shard_map/ppermute | solution.py:15
  107.0 21.5 %collective-permute-start.23 = (bf16[384,256]{0,1:T(8,128)(2,1)S(1)}, bf16[384,256]{0,1:T(8,128)(2,1)S(1)}, u32[]{:S(2)}, u32[]{:S(2)}) collective-permute-start(bf16[384,256]{0,1:T(8,128)(2,1)S(1)} %collective-permute-done.17), channel_id=1, source_target_pairs={{4,0},{8,4},{12,8},{16,12},{20,16},{24,20},{28,24},{32,28},{36,32}... | collective-permute-start | bytes 589832 | tf_op jit(solution)/shard_map/ppermute | solution.py:15
  108.9 20.3 %collective-permute-start.20 = (bf16[384,256]{0,1:T(8,128)(2,1)S(1)}, bf16[384,256]{0,1:T(8,128)(2,1)S(1)}, u32[]{:S(2)}, u32[]{:S(2)}) collective-permute-start(bf16[384,256]{0,1:T(8,128)(2,1)S(1)} %collective-permute-done.14), channel_id=1, source_target_pairs={{0,4},{4,8},{8,12},{12,16},{16,20},{20,24},{24,28},{28,32},{32,36}... | collective-permute-start | bytes 589832 | tf_op jit(solution)/shard_map/ppermute | solution.py:15
  129.2 1.0 copy-start.8
  131.6 80.3 %copy-start.11 = (f32[1024]{0:T(1024)S(1)}, f32[1024]{0:T(1024)}, u32[]{:S(2)}) copy-start(f32[1024]{0:T(1024)} %param.13) | copy-start | bytes 12292
  131.6 111.2 %reduce-scatter.2.cloned.1.call-start = ((), (), s32[]{:S(2)}) async-start(), calls=%async_computation.3 | async-start | bytes 983040 | tf_op jit(solution)/shard_map/reduce_scatter | solution.py:83
Sparse Core Ops, SparseCore 0:
  131.7 77.1 all-reduce.1
  219.8 22.8 reduce-scatter.1
